TPU v7x, 32 devices: a whole 2x2x4 slice. The times are simulated.
32 devices in a mesh: row: 4 (over y, core), col: 8 (over z, x).
Axes of the slice: x: 2, y: 2, z: 4, core: 2. Of those that a mesh axis runs over, the one named last changes fastest.
Arguments:
- embeddings: float32 [32768, 1024], P(('row', 'col')), may hold values from -6 to 6
- neighbour_ids: int32 [64, 12], P(('row', 'col')), may hold values from 0 to 63, as said below
- start_vectors: float32 [32768, 64], P(('row', 'col')), may hold values from -15 to 15
Outputs:
- spectral_vectors: float32 [32768, 64], P(('row', 'col'))
Inputs may be any that keep to these rules, and one draw needn't show every extreme that they name: `neighbour_ids`: slot 0 of block b is b itself. The other slots of block b name distinct blocks other than b held by devices of the same row index whose col index differs from that of b's device by at most 2 cyclically, followed by padding slots that repeat b. Block b sits on device b // 2, with device index row * 8 + col.
All inputs are finite; a program needn't handle non-finite values.
Results may differ from a plain program's by a relative error of at most 0.005.
Values may be sent and summed in bfloat16 or wider, within the bound.
No kernel may reach another device: no remote copies, remote signals or barrier semaphores. Data moves between devices by JAX's collectives and lax.ppermute only.
A program may use at most 128 MiB of HBM per device.

v0:
```python
import math
import jax
import jax.numpy as jnp
from jax import lax
from jax.sharding import PartitionSpec as P

D = 1024
BS = 512
SLOTS = 12
REACH = 2
ITERS = 3
BLK_DEV = 2
SHARP = 8.0
EPSILON = 1e-06


def passed_along(shard, axis, by):
    count = lax.axis_size(axis)
    return lax.ppermute(shard, axis, [(i, (i + by) % count) for i in range(count)])


def unit_rows(points):
    rms_inverse = lax.rsqrt(jnp.mean(points * points, axis=-1, keepdims=True) + EPSILON)
    return (points * rms_inverse).astype(jnp.bfloat16)


def band_index(neighbour_ids, col_count, col_index):
    holder = neighbour_ids // BLK_DEV
    offset = (holder % col_count - col_index + col_count + REACH) % col_count
    return offset * BLK_DEV + neighbour_ids % BLK_DEV


def assemble(pieces):
    return jnp.concatenate([pieces[offset] for offset in range(-REACH, REACH + 1)], axis=0)


def point_band(normed):
    pieces = {0: normed}
    for offset in [shifted for shifted in range(-REACH, REACH + 1) if shifted != 0]:
        pieces[offset] = passed_along(normed, "col", -offset)
    return assemble(pieces)


def vector_band(scaled):
    pieces = {0: scaled}
    for offset in [shifted for shifted in range(-REACH, REACH + 1) if shifted != 0]:
        pieces[offset] = passed_along(scaled, "col", -offset)
    return assemble(pieces)


def orthonormal(image_rows, total_rows):
    gram_sum = lax.dot_general(
        image_rows,
        image_rows,
        (((0,), (0,)), ((), ())),
        precision=lax.Precision.HIGHEST,
        preferred_element_type=jnp.float32,
    )
    gram_sum = lax.psum(gram_sum, ("row", "col"))
    factor = jnp.linalg.cholesky(gram_sum)
    solved = lax.linalg.triangular_solve(
        factor, image_rows, left_side=False, lower=True, transpose_a=True
    )
    return solved * math.sqrt(total_rows)


def on_device(embeddings, neighbour_ids, start_vectors):
    col_count = lax.axis_size("col")
    col_index = lax.axis_index("col")
    device = lax.axis_index("row") * col_count + col_index
    total_rows = embeddings.shape[0] * lax.axis_size("row") * col_count
    normed = unit_rows(embeddings)
    point_rows = point_band(normed)
    own_ids = device * BLK_DEV + jnp.arange(BLK_DEV, dtype=jnp.int32)
    slot_ids = jnp.arange(SLOTS, dtype=jnp.int32)
    live_mask = ((slot_ids[None, :] == 0) | (neighbour_ids != own_ids[:, None])).astype(jnp.float32)
    position = band_index(neighbour_ids, col_count, col_index)
    candidates = (2 * REACH + 1) * BLK_DEV
    own_blocks = normed.reshape(BLK_DEV, BS, D)
    tile_list = []
    degree_list = []
    chosen = jnp.sum(
        (position[:, :, None] == jnp.arange(candidates, dtype=jnp.int32)[None, None, :]).astype(
            jnp.float32
        )
        * live_mask[:, :, None],
        axis=1,
    )
    for member in range(BLK_DEV):
        cosine = (
            lax.dot_general(
                own_blocks[member],
                point_rows,
                (((1,), (1,)), ((), ())),
                preferred_element_type=jnp.float32,
            )
            / D
        )
        affinity = (
            jnp.exp(SHARP * (cosine - 1.0)).reshape(BS, candidates, BS)
            * chosen[member][None, :, None]
        )
        degree_list.append(jnp.sum(affinity, axis=(1, 2)))
        tile_list.append(affinity.reshape(BS, candidates * BS).astype(jnp.bfloat16))
    inv_root = lax.rsqrt(jnp.stack(degree_list))
    vectors = start_vectors
    for iteration in range(ITERS):
        scaled = (vectors * inv_root.reshape(-1, 1)).astype(jnp.bfloat16)
        spread = vector_band(scaled)
        image_list = []
        for member in range(BLK_DEV):
            partial_rows = jnp.dot(tile_list[member], spread, preferred_element_type=jnp.float32)
            image_list.append(partial_rows * inv_root[member][:, None])
        image_rows = jnp.concatenate(image_list, axis=0)
        vectors = orthonormal(image_rows, total_rows)
    return vectors


def solution(mesh):
    in_specs = (P(("row", "col"), None), P(("row", "col"), None), P(("row", "col"), None))
    out_specs = P(("row", "col"), None)
    return jax.shard_map(
        on_device, mesh=mesh, in_specs=in_specs, out_specs=out_specs, check_vma=False
    )
```

profile of v0, /device:TPU:0, one launch (start us, length us, event | category | flops | bytes accessed | tf_op | source)
XLA Modules:
  0.0 388.7 jit_solution(13238385011617048183)
XLA Ops:
  0.0 2.7 multiply_reduce_fusion
  2.7 0.7 copy-done.3
  3.5 1.6 multiply_convert_fusion
  5.1 3.1 collective-permute-start
  8.1 1.5 collective-permute-start.1
  9.6 3.2 collective-permute-start.2
  12.9 0.3 collective-permute-start.3
  13.2 0.1 fusion.23
  13.3 0.2 slice_reduce_fusion.1
  13.7 43.3 %collective-permute-done = bf16[1024,1024]{1,0:T(8,128)(2,1)} collective-permute-done((bf16[1024,1024]{1,0:T(8,128)(2,1)}, bf16[1024,1024]{1,0:T(8,128)(2,1)}, u32[]{:S(2)}, u32[]{:S(2)}) %collective-permute-start) | collective-permute-done | bytes 2097184 | tf_op jit(solution)/shard_map/ppermute | solution.py:19
  57.0 3.1 constant_dynamic-update-slice_fusion.4
  60.1 43.0 %collective-permute-done.1 = bf16[1024,1024]{1,0:T(8,128)(2,1)} collective-permute-done((bf16[1024,1024]{1,0:T(8,128)(2,1)}, bf16[1024,1024]{1,0:T(8,128)(2,1)}, u32[]{:S(2)}, u32[]{:S(2)}) %collective-permute-start.1) | collective-permute-done | bytes 2097184 | tf_op jit(solution)/shard_map/ppermute | solution.py:19
  103.1 3.1 constant_dynamic-update-slice_fusion.3
  106.2 1.6 constant_dynamic-update-slice_fusion.2
  107.8 3.2 constant_dynamic-update-slice_fusion.1
  111.0 34.9 %collective-permute-done.3 = bf16[1024,1024]{1,0:T(8,128)(2,1)S(1)} collective-permute-done((bf16[1024,1024]{1,0:T(8,128)(2,1)}, bf16[1024,1024]{1,0:T(8,128)(2,1)S(1)}, u32[]{:S(2)}, u32[]{:S(2)}) %collective-permute-start.3) | collective-permute-done | bytes 2097184 | tf_op jit(solution)/shard_map/ppermute | solution.py:19
  145.9 1.5 constant_dynamic-update-slice_fusion
  147.4 10.0 %fusion.45 = (f32[512]{0:T(512)S(1)}, bf16[512,5120]{1,0:T(8,128)(2,1)S(1)}) fusion(f32[5120]{0:T(1024)S(1)} %mul.152, bf16[5120,1024]{1,0:T(8,128)(2,1)} %constant_dynamic-update-slice_fusion, bf16[1024,1024]{1,0:T(8,128)(2,1)} %multiply_convert_fusion), kind=kOutput, calls=%fused_computation.114 | convolution fusion | flops 5384437248 | bytes 16799744 | tf_op jit(solution)/shard_map/dot_general | solution.py:91
  157.4 11.9 %fusion.44 = (f32[512]{0:T(512)S(1)}, bf16[512,5120]{1,0:T(8,128)(2,1)S(1)}) fusion(f32[5120]{0:T(1024)S(1)} %mul.158, bf16[5120,1024]{1,0:T(8,128)(2,1)} %constant_dynamic-update-slice_fusion, bf16[1024,1024]{1,0:T(8,128)(2,1)} %multiply_convert_fusion), kind=kOutput, calls=%fused_computation.113 | convolution fusion | flops 5384437248 | bytes 16799744 | tf_op jit(solution)/shard_map/dot_general | solution.py:91
  169.4 0.7 collective-permute-start.4
  170.1 1.5 collective-permute-start.5
  171.6 3.3 collective-permute-start.6
  174.8 10.5 %collective-permute-start.7 = (bf16[1024,64]{0,1:T(8,128)(2,1)S(1)}, bf16[1024,64]{0,1:T(8,128)(2,1)S(1)}, u32[]{:S(2)}, u32[]{:S(2)}) collective-permute-start(bf16[1024,64]{0,1:T(8,128)(2,1)S(1)} %multiply_convert_fusion.1), channel_id=1, source_target_pairs={{0,6},{1,7},{2,0},{3,1},{4,2},{5,3},{6,4},{7,5},{8,14},{9,15},{10,... | collective-permute-start | bytes 393224 | tf_op jit(solution)/shard_map/ppermute | solution.py:19
  185.4 0.9 collective-permute-done.6
  186.3 2.9 collective-permute-done.7
  189.1 1.7 convolution_multiply_fusion.5
  190.8 1.7 convolution_multiply_fusion.4
  192.6 0.4 fusion.9
  192.9 39.6 %psum.21 = f32[64,64]{0,1:T(8,128)S(1)} all-reduce(f32[64,64]{0,1:T(8,128)S(1)} %fusion.9), channel_id=1, replica_groups=mesh['row'=4,'col'=8] {'row','col'}, use_global_device_ids=true, to_apply=%region_4.5 | all-reduce | flops 4096 | bytes 32768 | tf_op jit(solution)/shard_map/psum | solution.py:59
  232.6 5.8 %cholesky.59 = f32[64,64]{1,0:T(8,128)S(1)} custom-call(f32[64,64]{1,0:T(8,128)S(1)} %fusion.18), custom_call_target="Cholesky" | custom-call | tf_op jit(solution)/shard_map/jit(cholesky)/cholesky | solution.py:60
  238.5 0.6 compare_reduce_fusion.2
  239.1 0.7 fusion.10
  239.8 4.9 %custom-call.7 = f32[1,64,64]{1,2,0:T(8,128)S(1)} custom-call(f32[1,64,64]{2,1,0:T(8,128)S(1)} %fusion.10), custom_call_target="InvertDiagBlocksLowerTriangular" | custom-call | tf_op jit(solution)/shard_map/triangular_solve/custom-call.0 | solution.py:61
  244.7 0.4 fusion.3
  245.1 1.2 collective-permute-start.8
  246.3 2.3 collective-permute-start.9
  248.5 2.5 collective-permute-start.10
  251.0 0.9 collective-permute-start.11
  251.9 0.9 collective-permute-done.8
  252.9 4.5 %collective-permute-done.9 = bf16[1024,64]{0,1:T(8,128)(2,1)S(1)} collective-permute-done((bf16[1024,64]{0,1:T(8,128)(2,1)S(1)}, bf16[1024,64]{0,1:T(8,128)(2,1)S(1)}, u32[]{:S(2)}, u32[]{:S(2)}) %collective-permute-start.9) | collective-permute-done | bytes 131104 | tf_op jit(solution)/shard_map/ppermute | solution.py:19
  257.5 4.2 %convolution_multiply_fusion.3 = f32[512,64]{0,1:T(8,128)S(1)} fusion(bf16[5120,64]{0,1:T(8,128)(2,1)S(1)} %constant_dynamic-update-slice_fusion.10, f32[512]{0:T(512)S(1)} %bitcast.68, bf16[512,5120]{1,0:T(8,128)(2,1)} %copy-done), kind=kOutput, calls=%fused_computation.15 | convolution fusion | flops 335577088 | bytes 6031360 | tf_op jit(solution)/shard_map/dot_general | solution.py:112
  261.7 1.7 convolution_multiply_fusion.2
  263.4 0.4 fusion.8
  263.8 38.8 %psum.22 = f32[64,64]{0,1:T(8,128)S(1)} all-reduce(f32[64,64]{0,1:T(8,128)S(1)} %fusion.8), channel_id=1, replica_groups=mesh['row'=4,'col'=8] {'row','col'}, use_global_device_ids=true, to_apply=%region_7.10 | all-reduce | flops 4096 | bytes 32768 | tf_op jit(solution)/shard_map/psum | solution.py:59
  302.7 5.8 %cholesky.70 = f32[64,64]{1,0:T(8,128)S(1)} custom-call(f32[64,64]{1,0:T(8,128)S(1)} %fusion.16), custom_call_target="Cholesky" | custom-call | tf_op jit(solution)/shard_map/jit(cholesky)/cholesky | solution.py:60
  308.6 0.6 compare_reduce_fusion.1
  309.2 0.7 fusion.11
  309.9 4.9 %custom-call.8 = f32[1,64,64]{1,2,0:T(8,128)S(1)} custom-call(f32[1,64,64]{2,1,0:T(8,128)S(1)} %fusion.11), custom_call_target="InvertDiagBlocksLowerTriangular" | custom-call | tf_op jit(solution)/shard_map/triangular_solve/custom-call.0 | solution.py:61
  314.8 0.4 fusion.4
  315.2 1.6 collective-permute-start.12
  316.8 2.3 collective-permute-start.13
  319.1 2.5 collective-permute-start.14
  321.5 0.5 collective-permute-start.15
  322.0 0.9 collective-permute-done.12
  323.0 4.5 %collective-permute-done.13 = bf16[1024,64]{0,1:T(8,128)(2,1)S(1)} collective-permute-done((bf16[1024,64]{0,1:T(8,128)(2,1)S(1)}, bf16[1024,64]{0,1:T(8,128)(2,1)S(1)}, u32[]{:S(2)}, u32[]{:S(2)}) %collective-permute-start.13) | collective-permute-done | bytes 131104 | tf_op jit(solution)/shard_map/ppermute | solution.py:19
  327.6 4.2 %convolution_multiply_fusion.1 = f32[512,64]{0,1:T(8,128)S(1)} fusion(bf16[5120,64]{0,1:T(8,128)(2,1)S(1)} %constant_dynamic-update-slice_fusion.15, f32[512]{0:T(512)S(1)} %bitcast.69, bf16[512,5120]{1,0:T(8,128)(2,1)} %copy-done), kind=kOutput, calls=%fused_computation.13 | convolution fusion | flops 335577088 | bytes 6031360 | tf_op jit(solution)/shard_map/dot_general | solution.py:112
  331.8 4.2 %convolution_multiply_fusion = f32[512,64]{0,1:T(8,128)S(1)} fusion(bf16[5120,64]{0,1:T(8,128)(2,1)S(1)} %constant_dynamic-update-slice_fusion.15, f32[512]{0:T(512)S(1)} %bitcast.66, bf16[512,5120]{1,0:T(8,128)(2,1)} %copy-done.1), kind=kOutput, calls=%fused_computation.12 | convolution fusion | flops 335577088 | bytes 6031360 | tf_op jit(solution)/shard_map/dot_general | solution.py:112
  336.0 0.4 fusion.7
  336.3 39.1 %psum.23 = f32[64,64]{0,1:T(8,128)S(1)} all-reduce(f32[64,64]{0,1:T(8,128)S(1)} %fusion.7), channel_id=1, replica_groups=mesh['row'=4,'col'=8] {'row','col'}, use_global_device_ids=true, to_apply=%region_8.11 | all-reduce | flops 4096 | bytes 32768 | tf_op jit(solution)/shard_map/psum | solution.py:59
  375.5 5.8 %cholesky.81 = f32[64,64]{1,0:T(8,128)S(1)} custom-call(f32[64,64]{1,0:T(8,128)S(1)} %fusion.14), custom_call_target="Cholesky" | custom-call | tf_op jit(solution)/shard_map/jit(cholesky)/cholesky | solution.py:60
  381.4 0.6 compare_reduce_fusion
  382.0 0.7 fusion.12
  382.7 4.9 %custom-call.9 = f32[1,64,64]{1,2,0:T(8,128)S(1)} custom-call(f32[1,64,64]{2,1,0:T(8,128)S(1)} %fusion.12), custom_call_target="InvertDiagBlocksLowerTriangular" | custom-call | tf_op jit(solution)/shard_map/triangular_solve/custom-call.0 | solution.py:61
  387.6 1.1 fusion
  (58 shorter events, 0.9 us)
Async XLA Ops:
  0.0 3.4 copy-start.3
  0.0 13.1 %copy-start.6 = (s32[2,12]{1,0:T(2,128)S(1)}, s32[2,12]{1,0:T(2,128)}, u32[]{:S(2)}) copy-start(s32[2,12]{1,0:T(2,128)} %param.7) | copy-start | bytes 292
  5.1 51.9 %collective-permute-start = (bf16[1024,1024]{1,0:T(8,128)(2,1)}, bf16[1024,1024]{1,0:T(8,128)(2,1)}, u32[]{:S(2)}, u32[]{:S(2)}) collective-permute-start(bf16[1024,1024]{1,0:T(8,128)(2,1)} %multiply_convert_fusion), channel_id=1, source_target_pairs={{0,2},{1,3},{2,4},{3,5},{4,6},{5,7},{6,0},{7,1},{8,10},{9,11},{10,... | collective-permute-start | bytes 6291464 | tf_op jit(solution)/shard_map/ppermute | solution.py:19
  8.1 94.9 %collective-permute-start.1 = (bf16[1024,1024]{1,0:T(8,128)(2,1)}, bf16[1024,1024]{1,0:T(8,128)(2,1)}, u32[]{:S(2)}, u32[]{:S(2)}) collective-permute-start(bf16[1024,1024]{1,0:T(8,128)(2,1)} %multiply_convert_fusion), channel_id=1, source_target_pairs={{0,1},{1,2},{2,3},{3,4},{4,5},{5,6},{6,7},{7,0},{8,9},{9,10},{10,1... | collective-permute-start | bytes 6291464 | tf_op jit(solution)/shard_map/ppermute | solution.py:19
  9.6 98.2 %collective-permute-start.2 = (bf16[1024,1024]{1,0:T(8,128)(2,1)}, bf16[1024,1024]{1,0:T(8,128)(2,1)}, u32[]{:S(2)}, u32[]{:S(2)}) collective-permute-start(bf16[1024,1024]{1,0:T(8,128)(2,1)} %multiply_convert_fusion), channel_id=1, source_target_pairs={{0,7},{1,0},{2,1},{3,2},{4,3},{5,4},{6,5},{7,6},{8,15},{9,8},{10,9... | collective-permute-start | bytes 6291464 | tf_op jit(solution)/shard_map/ppermute | solution.py:19
  12.9 133.0 %collective-permute-start.3 = (bf16[1024,1024]{1,0:T(8,128)(2,1)}, bf16[1024,1024]{1,0:T(8,128)(2,1)S(1)}, u32[]{:S(2)}, u32[]{:S(2)}) collective-permute-start(bf16[1024,1024]{1,0:T(8,128)(2,1)} %multiply_convert_fusion), channel_id=1, source_target_pairs={{0,6},{1,7},{2,0},{3,1},{4,2},{5,3},{6,4},{7,5},{8,14},{9,15},{10,... | collective-permute-start | bytes 6291464 | tf_op jit(solution)/shard_map/ppermute | solution.py:19
  13.7 92.5 %copy-start.4 = (f32[1024,1024]{1,0:T(8,128)S(1)}, f32[1024,1024]{1,0:T(8,128)}, u32[]{:S(2)}) copy-start(f32[1024,1024]{1,0:T(8,128)} %param.6) | copy-start | bytes 12582916
  157.4 31.7 %copy-start = (bf16[512,5120]{1,0:T(8,128)(2,1)}, bf16[512,5120]{1,0:T(8,128)(2,1)S(1)}, u32[]{:S(2)}) copy-start(bf16[512,5120]{1,0:T(8,128)(2,1)S(1)} %get-tuple-element.16) | copy-start | bytes 15728644
  157.4 12.0 %copy-start.5 = (f32[1024,64]{0,1:T(8,128)S(1)}, f32[1024,64]{0,1:T(8,128)}, u32[]{:S(2)}) copy-start(f32[1024,64]{0,1:T(8,128)} %param.8) | copy-start | bytes 786436
  169.4 23.2 %copy-start.1 = (bf16[512,5120]{1,0:T(8,128)(2,1)}, bf16[512,5120]{1,0:T(8,128)(2,1)S(1)}, u32[]{:S(2)}) copy-start(bf16[512,5120]{1,0:T(8,128)(2,1)S(1)} %get-tuple-element.14) | copy-start | bytes 15728644
  169.4 15.8 %collective-permute-start.4 = (bf16[1024,64]{0,1:T(8,128)(2,1)S(1)}, bf16[1024,64]{0,1:T(8,128)(2,1)S(1)}, u32[]{:S(2)}, u32[]{:S(2)}) collective-permute-start(bf16[1024,64]{0,1:T(8,128)(2,1)S(1)} %multiply_convert_fusion.1), channel_id=1, source_target_pairs={{0,2},{1,3},{2,4},{3,5},{4,6},{5,7},{6,0},{7,1},{8,10},{9,11},{10,... | collective-permute-start | bytes 393224 | tf_op jit(solution)/shard_map/ppermute | solution.py:19
  170.1 15.2 %collective-permute-start.5 = (bf16[1024,64]{0,1:T(8,128)(2,1)S(1)}, bf16[1024,64]{0,1:T(8,128)(2,1)S(1)}, u32[]{:S(2)}, u32[]{:S(2)}) collective-permute-start(bf16[1024,64]{0,1:T(8,128)(2,1)S(1)} %multiply_convert_fusion.1), channel_id=1, source_target_pairs={{0,1},{1,2},{2,3},{3,4},{4,5},{5,6},{6,7},{7,0},{8,9},{9,10},{10,1... | collective-permute-start | bytes 393224 | tf_op jit(solution)/shard_map/ppermute | solution.py:19
  171.6 14.7 %collective-permute-start.6 = (bf16[1024,64]{0,1:T(8,128)(2,1)S(1)}, bf16[1024,64]{0,1:T(8,128)(2,1)S(1)}, u32[]{:S(2)}, u32[]{:S(2)}) collective-permute-start(bf16[1024,64]{0,1:T(8,128)(2,1)S(1)} %multiply_convert_fusion.1), channel_id=1, source_target_pairs={{0,7},{1,0},{2,1},{3,2},{4,3},{5,4},{6,5},{7,6},{8,15},{9,8},{10,9... | collective-permute-start | bytes 393224 | tf_op jit(solution)/shard_map/ppermute | solution.py:19
  174.8 14.3 %collective-permute-start.7 = (bf16[1024,64]{0,1:T(8,128)(2,1)S(1)}, bf16[1024,64]{0,1:T(8,128)(2,1)S(1)}, u32[]{:S(2)}, u32[]{:S(2)}) collective-permute-start(bf16[1024,64]{0,1:T(8,128)(2,1)S(1)} %multiply_convert_fusion.1), channel_id=1, source_target_pairs={{0,6},{1,7},{2,0},{3,1},{4,2},{5,3},{6,4},{7,5},{8,14},{9,15},{10,... | collective-permute-start | bytes 393224 | tf_op jit(solution)/shard_map/ppermute | solution.py:19
  244.7 17.0 %copy-start.2 = (bf16[512,5120]{1,0:T(8,128)(2,1)S(1)}, bf16[512,5120]{1,0:T(8,128)(2,1)}, u32[]{:S(2)}) copy-start(bf16[512,5120]{1,0:T(8,128)(2,1)} %copy-done.1) | copy-start | bytes 15728644
  245.1 7.7 %collective-permute-start.8 = (bf16[1024,64]{0,1:T(8,128)(2,1)S(1)}, bf16[1024,64]{0,1:T(8,128)(2,1)S(1)}, u32[]{:S(2)}, u32[]{:S(2)}) collective-permute-start(bf16[1024,64]{0,1:T(8,128)(2,1)S(1)} %fusion.3), channel_id=1, source_target_pairs={{0,2},{1,3},{2,4},{3,5},{4,6},{5,7},{6,0},{7,1},{8,10},{9,11},{10,... | collective-permute-start | bytes 393224 | tf_op jit(solution)/shard_map/ppermute | solution.py:19
  246.3 11.1 %collective-permute-start.9 = (bf16[1024,64]{0,1:T(8,128)(2,1)S(1)}, bf16[1024,64]{0,1:T(8,128)(2,1)S(1)}, u32[]{:S(2)}, u32[]{:S(2)}) collective-permute-start(bf16[1024,64]{0,1:T(8,128)(2,1)S(1)} %fusion.3), channel_id=1, source_target_pairs={{0,1},{1,2},{2,3},{3,4},{4,5},{5,6},{6,7},{7,0},{8,9},{9,10},{10,1... | collective-permute-start | bytes 393224 | tf_op jit(solution)/shard_map/ppermute | solution.py:19
  248.5 8.9 %collective-permute-start.10 = (bf16[1024,64]{0,1:T(8,128)(2,1)S(1)}, bf16[1024,64]{0,1:T(8,128)(2,1)S(1)}, u32[]{:S(2)}, u32[]{:S(2)}) collective-permute-start(bf16[1024,64]{0,1:T(8,128)(2,1)S(1)} %fusion.3), channel_id=1, source_target_pairs={{0,7},{1,0},{2,1},{3,2},{4,3},{5,4},{6,5},{7,6},{8,15},{9,8},{10,9... | collective-permute-start | bytes 393224 | tf_op jit(solution)/shard_map/ppermute | solution.py:19
  251.0 6.5 %collective-permute-start.11 = (bf16[1024,64]{0,1:T(8,128)(2,1)S(1)}, bf16[1024,64]{0,1:T(8,128)(2,1)S(1)}, u32[]{:S(2)}, u32[]{:S(2)}) collective-permute-start(bf16[1024,64]{0,1:T(8,128)(2,1)S(1)} %fusion.3), channel_id=1, source_target_pairs={{0,6},{1,7},{2,0},{3,1},{4,2},{5,3},{6,4},{7,5},{8,14},{9,15},{10,... | collective-permute-start | bytes 393224 | tf_op jit(solution)/shard_map/ppermute | solution.py:19
  315.2 7.7 %collective-permute-start.12 = (bf16[1024,64]{0,1:T(8,128)(2,1)S(1)}, bf16[1024,64]{0,1:T(8,128)(2,1)S(1)}, u32[]{:S(2)}, u32[]{:S(2)}) collective-permute-start(bf16[1024,64]{0,1:T(8,128)(2,1)S(1)} %fusion.4), channel_id=1, source_target_pairs={{0,2},{1,3},{2,4},{3,5},{4,6},{5,7},{6,0},{7,1},{8,10},{9,11},{10,... | collective-permute-start | bytes 393224 | tf_op jit(solution)/shard_map/ppermute | solution.py:19
  316.8 10.7 %collective-permute-start.13 = (bf16[1024,64]{0,1:T(8,128)(2,1)S(1)}, bf16[1024,64]{0,1:T(8,128)(2,1)S(1)}, u32[]{:S(2)}, u32[]{:S(2)}) collective-permute-start(bf16[1024,64]{0,1:T(8,128)(2,1)S(1)} %fusion.4), channel_id=1, source_target_pairs={{0,1},{1,2},{2,3},{3,4},{4,5},{5,6},{6,7},{7,0},{8,9},{9,10},{10,1... | collective-permute-start | bytes 393224 | tf_op jit(solution)/shard_map/ppermute | solution.py:19
  319.1 8.5 %collective-permute-start.14 = (bf16[1024,64]{0,1:T(8,128)(2,1)S(1)}, bf16[1024,64]{0,1:T(8,128)(2,1)S(1)}, u32[]{:S(2)}, u32[]{:S(2)}) collective-permute-start(bf16[1024,64]{0,1:T(8,128)(2,1)S(1)} %fusion.4), channel_id=1, source_target_pairs={{0,7},{1,0},{2,1},{3,2},{4,3},{5,4},{6,5},{7,6},{8,15},{9,8},{10,9... | collective-permute-start | bytes 393224 | tf_op jit(solution)/shard_map/ppermute | solution.py:19
  321.5 6.0 %collective-permute-start.15 = (bf16[1024,64]{0,1:T(8,128)(2,1)S(1)}, bf16[1024,64]{0,1:T(8,128)(2,1)S(1)}, u32[]{:S(2)}, u32[]{:S(2)}) collective-permute-start(bf16[1024,64]{0,1:T(8,128)(2,1)S(1)} %fusion.4), channel_id=1, source_target_pairs={{0,6},{1,7},{2,0},{3,1},{4,2},{5,3},{6,4},{7,5},{8,14},{9,15},{10,... | collective-permute-start | bytes 393224 | tf_op jit(solution)/shard_map/ppermute | solution.py:19
where the time goes:
time: 389 us
  waiting for transfers between devices  136 us (35%)
  blocking collectives  117 us (30%)
  matrix products  42.8 us (11%)
  other arithmetic  42.4 us (11%)
  starting transfers between devices  37.5 us (10%)
  local copies, waits for them, and re-layouts  12.3 us (3%)
    ppermute x16, waiting for transfers between devices, passed_along(): lax.ppermute(shard, axis, [(i, (i + by) % count) for i in range(count)])  136 us
    psum x3, blocking collectives, orthonormal(): gram_sum = lax.psum(gram_sum, ('row', 'col'))  117 us
    ppermute x16, starting transfers between devices, passed_along(): lax.ppermute(shard, axis, [(i, (i + by) % count) for i in range(count)])  37.5 us
    dot_general x2, matrix products, on_device(): lax.dot_general(own_blocks[member], point_rows, (((1,), (1,)), ((), ())),...  22 us
    another operation x9, other arithmetic, orthonormal(): factor = jnp.linalg.cholesky(gram_sum)  19.6 us
    dot_general x6, matrix products, on_device(): jnp.dot(tile_list[member], spread, preferred_element_type=jnp.float32)  17.7 us
    another operation x6, other arithmetic, orthonormal(): lax.linalg.triangular_solve(factor, image_rows, left_side=False, lower=Tr...  16.6 us
    unnamed x29, local copies, waits for them, and re-layouts  10.2 us
  transfers between devices with their start and end apart: 16, of which 9 were waited for; matrix products, arithmetic and copies ran while one was open for 3% of the time, Pallas kernels for 0%

commit v1 on v0

--- a/solution.py
+++ b/solution.py
@@ -56,7 +56,7 @@
         precision=lax.Precision.HIGHEST,
         preferred_element_type=jnp.float32,
     )
-    gram_sum = lax.psum(gram_sum, ("row", "col"))
+    gram_sum = lax.psum(lax.psum(gram_sum, "col"), "row")
     factor = jnp.linalg.cholesky(gram_sum)
     solved = lax.linalg.triangular_solve(
         factor, image_rows, left_side=False, lower=True, transpose_a=True

time: 389 us -> 406 us (1.044)
  blocking collectives: 117 us -> 138 us
    psum x3 -> x6, blocking collectives: 117 us -> 138 us  [orthonormal(): gram_sum = lax.psum(lax.psum(gram_sum, 'col'), 'row')]
  transfers between devices with their start and end apart: 16 -> 16, of which waited for: 9 -> 11; matrix products, arithmetic and copies ran while one was open for 3% -> 3% of each run, Pallas kernels for 0% -> 0%
where the time goes in v1:
time: 406 us
  blocking collectives  138 us (34%)
  waiting for transfers between devices  133 us (33%)
  matrix products  42.8 us (11%)
  other arithmetic  42.4 us (10%)
  starting transfers between devices  37.4 us (9%)
  local copies, waits for them, and re-layouts  12.3 us (3%)
    psum x6, blocking collectives, orthonormal(): gram_sum = lax.psum(lax.psum(gram_sum, 'col'), 'row')  138 us
    ppermute x16, waiting for transfers between devices, passed_along(): lax.ppermute(shard, axis, [(i, (i + by) % count) for i in range(count)])  133 us
    ppermute x16, starting transfers between devices, passed_along(): lax.ppermute(shard, axis, [(i, (i + by) % count) for i in range(count)])  37.4 us
    dot_general x2, matrix products, on_device(): lax.dot_general(own_blocks[member], point_rows, (((1,), (1,)), ((), ())),...  22 us
    another operation x9, other arithmetic, orthonormal(): factor = jnp.linalg.cholesky(gram_sum)  19.6 us
    dot_general x6, matrix products, on_device(): jnp.dot(tile_list[member], spread, preferred_element_type=jnp.float32)  17.7 us
    another operation x6, other arithmetic, orthonormal(): lax.linalg.triangular_solve(factor, image_rows, left_side=False, lower=Tr...  16.6 us
    unnamed x29, local copies, waits for them, and re-layouts  10.2 us
  transfers between devices with their start and end apart: 16, of which 11 were waited for; matrix products, arithmetic and copies ran while one was open for 3% of the time, Pallas kernels for 0%

profile of v1, /device:TPU:0, one launch (start us, length us, event | category | flops | bytes accessed | tf_op | source)
XLA Modules:
  0.0 405.8 jit_solution(17831062169499786472)
XLA Ops:
  0.0 2.7 multiply_reduce_fusion
  2.7 0.7 copy-done.3
  3.5 1.6 multiply_convert_fusion
  5.1 3.1 collective-permute-start
  8.1 1.5 collective-permute-start.1
  9.6 3.2 collective-permute-start.2
  12.9 0.3 collective-permute-start.3
  13.3 0.2 slice_reduce_fusion.1
  13.7 43.3 %collective-permute-done = bf16[1024,1024]{1,0:T(8,128)(2,1)} collective-permute-done((bf16[1024,1024]{1,0:T(8,128)(2,1)}, bf16[1024,1024]{1,0:T(8,128)(2,1)}, u32[]{:S(2)}, u32[]{:S(2)}) %collective-permute-start) | collective-permute-done | bytes 2097184 | tf_op jit(solution)/shard_map/ppermute | solution.py:19
  57.0 3.1 constant_dynamic-update-slice_fusion.4
  60.1 43.0 %collective-permute-done.1 = bf16[1024,1024]{1,0:T(8,128)(2,1)} collective-permute-done((bf16[1024,1024]{1,0:T(8,128)(2,1)}, bf16[1024,1024]{1,0:T(8,128)(2,1)}, u32[]{:S(2)}, u32[]{:S(2)}) %collective-permute-start.1) | collective-permute-done | bytes 2097184 | tf_op jit(solution)/shard_map/ppermute | solution.py:19
  103.1 3.1 constant_dynamic-update-slice_fusion.3
  106.2 1.6 constant_dynamic-update-slice_fusion.2
  107.8 3.2 constant_dynamic-update-slice_fusion.1
  111.0 34.9 %collective-permute-done.3 = bf16[1024,1024]{1,0:T(8,128)(2,1)S(1)} collective-permute-done((bf16[1024,1024]{1,0:T(8,128)(2,1)}, bf16[1024,1024]{1,0:T(8,128)(2,1)S(1)}, u32[]{:S(2)}, u32[]{:S(2)}) %collective-permute-start.3) | collective-permute-done | bytes 2097184 | tf_op jit(solution)/shard_map/ppermute | solution.py:19
  145.9 1.5 constant_dynamic-update-slice_fusion
  147.4 10.0 %fusion.45 = (f32[512]{0:T(512)S(1)}, bf16[512,5120]{1,0:T(8,128)(2,1)S(1)}) fusion(f32[5120]{0:T(1024)S(1)} %mul.152, bf16[5120,1024]{1,0:T(8,128)(2,1)} %constant_dynamic-update-slice_fusion, bf16[1024,1024]{1,0:T(8,128)(2,1)} %multiply_convert_fusion), kind=kOutput, calls=%fused_computation.114 | convolution fusion | flops 5384437248 | bytes 16799744 | tf_op jit(solution)/shard_map/dot_general | solution.py:91
  157.4 11.9 %fusion.44 = (f32[512]{0:T(512)S(1)}, bf16[512,5120]{1,0:T(8,128)(2,1)S(1)}) fusion(f32[5120]{0:T(1024)S(1)} %mul.158, bf16[5120,1024]{1,0:T(8,128)(2,1)} %constant_dynamic-update-slice_fusion, bf16[1024,1024]{1,0:T(8,128)(2,1)} %multiply_convert_fusion), kind=kOutput, calls=%fused_computation.113 | convolution fusion | flops 5384437248 | bytes 16799744 | tf_op jit(solution)/shard_map/dot_general | solution.py:91
  169.4 0.7 collective-permute-start.4
  170.1 1.5 collective-permute-start.5
  171.6 3.3 collective-permute-start.6
  174.8 10.5 %collective-permute-start.7 = (bf16[1024,64]{0,1:T(8,128)(2,1)S(1)}, bf16[1024,64]{0,1:T(8,128)(2,1)S(1)}, u32[]{:S(2)}, u32[]{:S(2)}) collective-permute-start(bf16[1024,64]{0,1:T(8,128)(2,1)S(1)} %multiply_convert_fusion.1), channel_id=1, source_target_pairs={{0,6},{1,7},{2,0},{3,1},{4,2},{5,3},{6,4},{7,5},{8,14},{9,15},{10,... | collective-permute-start | bytes 393224 | tf_op jit(solution)/shard_map/ppermute | solution.py:19
  185.4 0.9 collective-permute-done.6
  186.3 2.9 collective-permute-done.7
  189.1 1.7 convolution_multiply_fusion.5
  190.8 1.7 convolution_multiply_fusion.4
  192.6 0.4 fusion.9
  192.9 34.8 %psum.42 = f32[64,64]{0,1:T(8,128)S(1)} all-reduce(f32[64,64]{0,1:T(8,128)S(1)} %fusion.9), channel_id=1, replica_groups=mesh['row'=4,'col'=8] {'col'}, use_global_device_ids=true, to_apply=%region_4.5 | all-reduce | flops 4096 | bytes 32768 | tf_op jit(solution)/shard_map/psum | solution.py:59
  227.7 10.3 %psum.43 = f32[64,64]{0,1:T(8,128)S(1)} all-reduce(f32[64,64]{0,1:T(8,128)S(1)} %psum.42), channel_id=1, replica_groups=mesh['row'=4,'col'=8] {'row'}, use_global_device_ids=true, to_apply=%region_5.6 | all-reduce | flops 4096 | bytes 32768 | tf_op jit(solution)/shard_map/psum | solution.py:59
  238.1 5.8 %cholesky.59 = f32[64,64]{1,0:T(8,128)S(1)} custom-call(f32[64,64]{1,0:T(8,128)S(1)} %fusion.18), custom_call_target="Cholesky" | custom-call | tf_op jit(solution)/shard_map/jit(cholesky)/cholesky | solution.py:60
  244.0 0.6 compare_reduce_fusion.2
  244.6 0.7 fusion.10
  245.3 4.9 %custom-call.7 = f32[1,64,64]{1,2,0:T(8,128)S(1)} custom-call(f32[1,64,64]{2,1,0:T(8,128)S(1)} %fusion.10), custom_call_target="InvertDiagBlocksLowerTriangular" | custom-call | tf_op jit(solution)/shard_map/triangular_solve/custom-call.0 | solution.py:61
  250.2 0.4 fusion.3
  250.7 4.7 %collective-permute-start.10 = (bf16[1024,64]{0,1:T(8,128)(2,1)S(1)}, bf16[1024,64]{0,1:T(8,128)(2,1)S(1)}, u32[]{:S(2)}, u32[]{:S(2)}) collective-permute-start(bf16[1024,64]{0,1:T(8,128)(2,1)S(1)} %fusion.3), channel_id=1, source_target_pairs={{0,7},{1,0},{2,1},{3,2},{4,3},{5,4},{6,5},{7,6},{8,15},{9,8},{10,9... | collective-permute-start | bytes 393224 | tf_op jit(solution)/shard_map/ppermute | solution.py:19
  255.4 2.0 collective-permute-start.11
  257.4 1.1 collective-permute-done.8
  258.5 1.3 collective-permute-done.9
  259.9 1.4 collective-permute-done.11
  261.3 4.2 %convolution_multiply_fusion.3 = f32[512,64]{0,1:T(8,128)S(1)} fusion(bf16[5120,64]{0,1:T(8,128)(2,1)S(1)} %constant_dynamic-update-slice_fusion.10, f32[512]{0:T(512)S(1)} %bitcast.68, bf16[512,5120]{1,0:T(8,128)(2,1)} %copy-done), kind=kOutput, calls=%fused_computation.15 | convolution fusion | flops 335577088 | bytes 6031360 | tf_op jit(solution)/shard_map/dot_general | solution.py:112
  265.5 1.7 convolution_multiply_fusion.2
  267.2 0.4 fusion.8
  267.6 36.1 %psum.44 = f32[64,64]{0,1:T(8,128)S(1)} all-reduce(f32[64,64]{0,1:T(8,128)S(1)} %fusion.8), channel_id=1, replica_groups=mesh['row'=4,'col'=8] {'col'}, use_global_device_ids=true, to_apply=%region_8.11 | all-reduce | flops 4096 | bytes 32768 | tf_op jit(solution)/shard_map/psum | solution.py:59
  303.7 10.3 %psum.45 = f32[64,64]{0,1:T(8,128)S(1)} all-reduce(f32[64,64]{0,1:T(8,128)S(1)} %psum.44), channel_id=1, replica_groups=mesh['row'=4,'col'=8] {'row'}, use_global_device_ids=true, to_apply=%region_9.12 | all-reduce | flops 4096 | bytes 32768 | tf_op jit(solution)/shard_map/psum | solution.py:59
  314.1 5.8 %cholesky.70 = f32[64,64]{1,0:T(8,128)S(1)} custom-call(f32[64,64]{1,0:T(8,128)S(1)} %fusion.16), custom_call_target="Cholesky" | custom-call | tf_op jit(solution)/shard_map/jit(cholesky)/cholesky | solution.py:60
  319.9 0.6 compare_reduce_fusion.1
  320.6 0.7 fusion.11
  321.2 4.9 %custom-call.8 = f32[1,64,64]{1,2,0:T(8,128)S(1)} custom-call(f32[1,64,64]{2,1,0:T(8,128)S(1)} %fusion.11), custom_call_target="InvertDiagBlocksLowerTriangular" | custom-call | tf_op jit(solution)/shard_map/triangular_solve/custom-call.0 | solution.py:61
  326.1 0.4 fusion.4
  326.7 4.7 %collective-permute-start.14 = (bf16[1024,64]{0,1:T(8,128)(2,1)S(1)}, bf16[1024,64]{0,1:T(8,128)(2,1)S(1)}, u32[]{:S(2)}, u32[]{:S(2)}) collective-permute-start(bf16[1024,64]{0,1:T(8,128)(2,1)S(1)} %fusion.4), channel_id=1, source_target_pairs={{0,7},{1,0},{2,1},{3,2},{4,3},{5,4},{6,5},{7,6},{8,15},{9,8},{10,9... | collective-permute-start | bytes 393224 | tf_op jit(solution)/shard_map/ppermute | solution.py:19
  331.4 2.0 collective-permute-start.15
  333.4 1.1 collective-permute-done.12
  334.5 1.3 collective-permute-done.13
  335.8 1.4 collective-permute-done.15
  337.3 4.2 %convolution_multiply_fusion.1 = f32[512,64]{0,1:T(8,128)S(1)} fusion(bf16[5120,64]{0,1:T(8,128)(2,1)S(1)} %constant_dynamic-update-slice_fusion.15, f32[512]{0:T(512)S(1)} %bitcast.69, bf16[512,5120]{1,0:T(8,128)(2,1)} %copy-done), kind=kOutput, calls=%fused_computation.13 | convolution fusion | flops 335577088 | bytes 6031360 | tf_op jit(solution)/shard_map/dot_general | solution.py:112
  341.5 4.2 %convolution_multiply_fusion = f32[512,64]{0,1:T(8,128)S(1)} fusion(bf16[5120,64]{0,1:T(8,128)(2,1)S(1)} %constant_dynamic-update-slice_fusion.15, f32[512]{0:T(512)S(1)} %bitcast.66, bf16[512,5120]{1,0:T(8,128)(2,1)} %copy-done.1), kind=kOutput, calls=%fused_computation.12 | convolution fusion | flops 335577088 | bytes 6031360 | tf_op jit(solution)/shard_map/dot_general | solution.py:112
  345.7 0.4 fusion.7
  346.0 36.2 %psum.46 = f32[64,64]{0,1:T(8,128)S(1)} all-reduce(f32[64,64]{0,1:T(8,128)S(1)} %fusion.7), channel_id=1, replica_groups=mesh['row'=4,'col'=8] {'col'}, use_global_device_ids=true, to_apply=%region_10.13 | all-reduce | flops 4096 | bytes 32768 | tf_op jit(solution)/shard_map/psum | solution.py:59
  382.2 10.3 %psum.47 = f32[64,64]{0,1:T(8,128)S(1)} all-reduce(f32[64,64]{0,1:T(8,128)S(1)} %psum.46), channel_id=1, replica_groups=mesh['row'=4,'col'=8] {'row'}, use_global_device_ids=true, to_apply=%region_11.14 | all-reduce | flops 4096 | bytes 32768 | tf_op jit(solution)/shard_map/psum | solution.py:59
  392.6 5.8 %cholesky.81 = f32[64,64]{1,0:T(8,128)S(1)} custom-call(f32[64,64]{1,0:T(8,128)S(1)} %fusion.14), custom_call_target="Cholesky" | custom-call | tf_op jit(solution)/shard_map/jit(cholesky)/cholesky | solution.py:60
  398.4 0.6 compare_reduce_fusion
  399.1 0.7 fusion.12
  399.7 4.9 %custom-call.9 = f32[1,64,64]{1,2,0:T(8,128)S(1)} custom-call(f32[1,64,64]{2,1,0:T(8,128)S(1)} %fusion.12), custom_call_target="InvertDiagBlocksLowerTriangular" | custom-call | tf_op jit(solution)/shard_map/triangular_solve/custom-call.0 | solution.py:61
  404.6 1.1 fusion
  (61 shorter events, 1.2 us)
Async XLA Ops:
  0.0 3.4 copy-start.3
  0.0 13.1 %copy-start.6 = (s32[2,12]{1,0:T(2,128)S(1)}, s32[2,12]{1,0:T(2,128)}, u32[]{:S(2)}) copy-start(s32[2,12]{1,0:T(2,128)} %param.7) | copy-start | bytes 292
  5.1 51.9 %collective-permute-start = (bf16[1024,1024]{1,0:T(8,128)(2,1)}, bf16[1024,1024]{1,0:T(8,128)(2,1)}, u32[]{:S(2)}, u32[]{:S(2)}) collective-permute-start(bf16[1024,1024]{1,0:T(8,128)(2,1)} %multiply_convert_fusion), channel_id=1, source_target_pairs={{0,2},{1,3},{2,4},{3,5},{4,6},{5,7},{6,0},{7,1},{8,10},{9,11},{10,... | collective-permute-start | bytes 6291464 | tf_op jit(solution)/shard_map/ppermute | solution.py:19
  8.1 94.9 %collective-permute-start.1 = (bf16[1024,1024]{1,0:T(8,128)(2,1)}, bf16[1024,1024]{1,0:T(8,128)(2,1)}, u32[]{:S(2)}, u32[]{:S(2)}) collective-permute-start(bf16[1024,1024]{1,0:T(8,128)(2,1)} %multiply_convert_fusion), channel_id=1, source_target_pairs={{0,1},{1,2},{2,3},{3,4},{4,5},{5,6},{6,7},{7,0},{8,9},{9,10},{10,1... | collective-permute-start | bytes 6291464 | tf_op jit(solution)/shard_map/ppermute | solution.py:19
  9.6 98.2 %collective-permute-start.2 = (bf16[1024,1024]{1,0:T(8,128)(2,1)}, bf16[1024,1024]{1,0:T(8,128)(2,1)}, u32[]{:S(2)}, u32[]{:S(2)}) collective-permute-start(bf16[1024,1024]{1,0:T(8,128)(2,1)} %multiply_convert_fusion), channel_id=1, source_target_pairs={{0,7},{1,0},{2,1},{3,2},{4,3},{5,4},{6,5},{7,6},{8,15},{9,8},{10,9... | collective-permute-start | bytes 6291464 | tf_op jit(solution)/shard_map/ppermute | solution.py:19
  12.9 133.0 %collective-permute-start.3 = (bf16[1024,1024]{1,0:T(8,128)(2,1)}, bf16[1024,1024]{1,0:T(8,128)(2,1)S(1)}, u32[]{:S(2)}, u32[]{:S(2)}) collective-permute-start(bf16[1024,1024]{1,0:T(8,128)(2,1)} %multiply_convert_fusion), channel_id=1, source_target_pairs={{0,6},{1,7},{2,0},{3,1},{4,2},{5,3},{6,4},{7,5},{8,14},{9,15},{10,... | collective-permute-start | bytes 6291464 | tf_op jit(solution)/shard_map/ppermute | solution.py:19
  13.7 92.5 %copy-start.4 = (f32[1024,1024]{1,0:T(8,128)S(1)}, f32[1024,1024]{1,0:T(8,128)}, u32[]{:S(2)}) copy-start(f32[1024,1024]{1,0:T(8,128)} %param.6) | copy-start | bytes 12582916
  157.4 31.7 %copy-start = (bf16[512,5120]{1,0:T(8,128)(2,1)}, bf16[512,5120]{1,0:T(8,128)(2,1)S(1)}, u32[]{:S(2)}) copy-start(bf16[512,5120]{1,0:T(8,128)(2,1)S(1)} %get-tuple-element.16) | copy-start | bytes 15728644
  157.4 12.0 %copy-start.5 = (f32[1024,64]{0,1:T(8,128)S(1)}, f32[1024,64]{0,1:T(8,128)}, u32[]{:S(2)}) copy-start(f32[1024,64]{0,1:T(8,128)} %param.8) | copy-start | bytes 786436
  169.4 23.2 %copy-start.1 = (bf16[512,5120]{1,0:T(8,128)(2,1)}, bf16[512,5120]{1,0:T(8,128)(2,1)S(1)}, u32[]{:S(2)}) copy-start(bf16[512,5120]{1,0:T(8,128)(2,1)S(1)} %get-tuple-element.14) | copy-start | bytes 15728644
  169.4 15.8 %collective-permute-start.4 = (bf16[1024,64]{0,1:T(8,128)(2,1)S(1)}, bf16[1024,64]{0,1:T(8,128)(2,1)S(1)}, u32[]{:S(2)}, u32[]{:S(2)}) collective-permute-start(bf16[1024,64]{0,1:T(8,128)(2,1)S(1)} %multiply_convert_fusion.1), channel_id=1, source_target_pairs={{0,2},{1,3},{2,4},{3,5},{4,6},{5,7},{6,0},{7,1},{8,10},{9,11},{10,... | collective-permute-start | bytes 393224 | tf_op jit(solution)/shard_map/ppermute | solution.py:19
  170.1 15.2 %collective-permute-start.5 = (bf16[1024,64]{0,1:T(8,128)(2,1)S(1)}, bf16[1024,64]{0,1:T(8,128)(2,1)S(1)}, u32[]{:S(2)}, u32[]{:S(2)}) collective-permute-start(bf16[1024,64]{0,1:T(8,128)(2,1)S(1)} %multiply_convert_fusion.1), channel_id=1, source_target_pairs={{0,1},{1,2},{2,3},{3,4},{4,5},{5,6},{6,7},{7,0},{8,9},{9,10},{10,1... | collective-permute-start | bytes 393224 | tf_op jit(solution)/shard_map/ppermute | solution.py:19
  171.6 14.7 %collective-permute-start.6 = (bf16[1024,64]{0,1:T(8,128)(2,1)S(1)}, bf16[1024,64]{0,1:T(8,128)(2,1)S(1)}, u32[]{:S(2)}, u32[]{:S(2)}) collective-permute-start(bf16[1024,64]{0,1:T(8,128)(2,1)S(1)} %multiply_convert_fusion.1), channel_id=1, source_target_pairs={{0,7},{1,0},{2,1},{3,2},{4,3},{5,4},{6,5},{7,6},{8,15},{9,8},{10,9... | collective-permute-start | bytes 393224 | tf_op jit(solution)/shard_map/ppermute | solution.py:19
  174.8 14.3 %collective-permute-start.7 = (bf16[1024,64]{0,1:T(8,128)(2,1)S(1)}, bf16[1024,64]{0,1:T(8,128)(2,1)S(1)}, u32[]{:S(2)}, u32[]{:S(2)}) collective-permute-start(bf16[1024,64]{0,1:T(8,128)(2,1)S(1)} %multiply_convert_fusion.1), channel_id=1, source_target_pairs={{0,6},{1,7},{2,0},{3,1},{4,2},{5,3},{6,4},{7,5},{8,14},{9,15},{10,... | collective-permute-start | bytes 393224 | tf_op jit(solution)/shard_map/ppermute | solution.py:19
  250.2 15.3 %copy-start.2 = (bf16[512,5120]{1,0:T(8,128)(2,1)S(1)}, bf16[512,5120]{1,0:T(8,128)(2,1)}, u32[]{:S(2)}) copy-start(bf16[512,5120]{1,0:T(8,128)(2,1)} %copy-done.1) | copy-start | bytes 15728644
  250.6 7.9 %collective-permute-start.8 = (bf16[1024,64]{0,1:T(8,128)(2,1)S(1)}, bf16[1024,64]{0,1:T(8,128)(2,1)S(1)}, u32[]{:S(2)}, u32[]{:S(2)}) collective-permute-start(bf16[1024,64]{0,1:T(8,128)(2,1)S(1)} %fusion.3), channel_id=1, source_target_pairs={{0,2},{1,3},{2,4},{3,5},{4,6},{5,7},{6,0},{7,1},{8,10},{9,11},{10,... | collective-permute-start | bytes 393224 | tf_op jit(solution)/shard_map/ppermute | solution.py:19
  250.7 9.2 %collective-permute-start.9 = (bf16[1024,64]{0,1:T(8,128)(2,1)S(1)}, bf16[1024,64]{0,1:T(8,128)(2,1)S(1)}, u32[]{:S(2)}, u32[]{:S(2)}) collective-permute-start(bf16[1024,64]{0,1:T(8,128)(2,1)S(1)} %fusion.3), channel_id=1, source_target_pairs={{0,1},{1,2},{2,3},{3,4},{4,5},{5,6},{6,7},{7,0},{8,9},{9,10},{10,1... | collective-permute-start | bytes 393224 | tf_op jit(solution)/shard_map/ppermute | solution.py:19
  250.7 9.1 %collective-permute-start.10 = (bf16[1024,64]{0,1:T(8,128)(2,1)S(1)}, bf16[1024,64]{0,1:T(8,128)(2,1)S(1)}, u32[]{:S(2)}, u32[]{:S(2)}) collective-permute-start(bf16[1024,64]{0,1:T(8,128)(2,1)S(1)} %fusion.3), channel_id=1, source_target_pairs={{0,7},{1,0},{2,1},{3,2},{4,3},{5,4},{6,5},{7,6},{8,15},{9,8},{10,9... | collective-permute-start | bytes 393224 | tf_op jit(solution)/shard_map/ppermute | solution.py:19
  255.4 5.8 %collective-permute-start.11 = (bf16[1024,64]{0,1:T(8,128)(2,1)S(1)}, bf16[1024,64]{0,1:T(8,128)(2,1)S(1)}, u32[]{:S(2)}, u32[]{:S(2)}) collective-permute-start(bf16[1024,64]{0,1:T(8,128)(2,1)S(1)} %fusion.3), channel_id=1, source_target_pairs={{0,6},{1,7},{2,0},{3,1},{4,2},{5,3},{6,4},{7,5},{8,14},{9,15},{10,... | collective-permute-start | bytes 393224 | tf_op jit(solution)/shard_map/ppermute | solution.py:19
  326.6 7.9 %collective-permute-start.12 = (bf16[1024,64]{0,1:T(8,128)(2,1)S(1)}, bf16[1024,64]{0,1:T(8,128)(2,1)S(1)}, u32[]{:S(2)}, u32[]{:S(2)}) collective-permute-start(bf16[1024,64]{0,1:T(8,128)(2,1)S(1)} %fusion.4), channel_id=1, source_target_pairs={{0,2},{1,3},{2,4},{3,5},{4,6},{5,7},{6,0},{7,1},{8,10},{9,11},{10,... | collective-permute-start | bytes 393224 | tf_op jit(solution)/shard_map/ppermute | solution.py:19
  326.6 9.1 %collective-permute-start.13 = (bf16[1024,64]{0,1:T(8,128)(2,1)S(1)}, bf16[1024,64]{0,1:T(8,128)(2,1)S(1)}, u32[]{:S(2)}, u32[]{:S(2)}) collective-permute-start(bf16[1024,64]{0,1:T(8,128)(2,1)S(1)} %fusion.4), channel_id=1, source_target_pairs={{0,1},{1,2},{2,3},{3,4},{4,5},{5,6},{6,7},{7,0},{8,9},{9,10},{10,1... | collective-permute-start | bytes 393224 | tf_op jit(solution)/shard_map/ppermute | solution.py:19
  326.7 9.1 %collective-permute-start.14 = (bf16[1024,64]{0,1:T(8,128)(2,1)S(1)}, bf16[1024,64]{0,1:T(8,128)(2,1)S(1)}, u32[]{:S(2)}, u32[]{:S(2)}) collective-permute-start(bf16[1024,64]{0,1:T(8,128)(2,1)S(1)} %fusion.4), channel_id=1, source_target_pairs={{0,7},{1,0},{2,1},{3,2},{4,3},{5,4},{6,5},{7,6},{8,15},{9,8},{10,9... | collective-permute-start | bytes 393224 | tf_op jit(solution)/shard_map/ppermute | solution.py:19
  331.4 5.8 %collective-permute-start.15 = (bf16[1024,64]{0,1:T(8,128)(2,1)S(1)}, bf16[1024,64]{0,1:T(8,128)(2,1)S(1)}, u32[]{:S(2)}, u32[]{:S(2)}) collective-permute-start(bf16[1024,64]{0,1:T(8,128)(2,1)S(1)} %fusion.4), channel_id=1, source_target_pairs={{0,6},{1,7},{2,0},{3,1},{4,2},{5,3},{6,4},{7,5},{8,14},{9,15},{10,... | collective-permute-start | bytes 393224 | tf_op jit(solution)/shard_map/ppermute | solution.py:19
